TPU v7x, 128 devices: a whole 4x4x4 slice. The times are simulated.
128 devices in a mesh: pos: 16 (over x, z), tile: 8 (over y, core).
Axes of the slice: x: 4, y: 4, z: 4, core: 2. Of those that a mesh axis runs over, the one named last changes fastest.
Arguments:
- probe_modes: float32 [8, 2, 256, 256], P('tile'), may hold values from -1.1 to 1.1
- object_slices: bfloat16 [2, 2, 512, 2048], P(None, None, 'tile'), may hold values from -6 to 6
- amplitudes: bfloat16 [128, 256, 256], P('pos'), may hold values from 0.5 to 3
- scan_offsets: int32 [128, 2], replicated, may hold values from 0 to 1792, as said below
- slot_counts: int32 [16], replicated, may hold values from 1 to 8, 64 in all
Outputs:
- object_grad: float32 [2, 2, 512, 2048], P(None, None, 'tile', 'pos')
- probe_grad: float32 [8, 2, 256, 256], P('tile', None, 'pos')
Inputs may be any that keep to these rules, and one draw needn't show every extreme that they name: slot_counts[g] is how many leading slots of group g are live scan positions; the counts sum to 64 and the largest is exactly 8. scan_offsets[s] is (row, column); the row is at most 256 and the column at most 1792, both reached in every draw.
All inputs are finite; a program needn't handle non-finite values.
Results may differ from a plain program's by a relative error of at most 0.025.
Values may be sent and summed in bfloat16 or wider, within the bound.
A program may use at most 128 MiB of HBM per device.

v0:
```python
import jax
import jax.numpy as jnp
from jax import lax
from jax.sharding import PartitionSpec as P

FRESNEL = 0.37


def make_tables(points):
    counter = jnp.arange(points, dtype=jnp.int32)
    product = counter[:, None] * counter[None, :] % points
    angle = 2.0 * jnp.pi / points * product.astype(jnp.float32)
    factor = 1.0 / jnp.sqrt(jnp.float32(points))
    table_re = (jnp.cos(angle) * factor).astype(jnp.bfloat16)
    table_im = (-jnp.sin(angle) * factor).astype(jnp.bfloat16)
    shifted = ((counter + points // 2) % points - points // 2).astype(jnp.float32)
    phase = (
        jnp.pi
        * FRESNEL
        / points
        * (shifted[:, None] * shifted[:, None] + shifted[None, :] * shifted[None, :])
    )
    kernel = jnp.stack([jnp.cos(phase), -jnp.sin(phase)])
    return (table_re, table_im, kernel)


def times_complex(first, second):
    real_part = (
        first[..., 0, :, :] * second[..., 0, :, :] - first[..., 1, :, :] * second[..., 1, :, :]
    )
    imag_part = (
        first[..., 0, :, :] * second[..., 1, :, :] + first[..., 1, :, :] * second[..., 0, :, :]
    )
    return jnp.stack([real_part, imag_part], axis=-3)


def conjugate(values):
    return jnp.stack([values[..., 0, :, :], -values[..., 1, :, :]], axis=-3)


def transform_many(values, table_re, table_im):
    tables = jnp.stack([table_re, table_im])
    lowered = values.astype(jnp.bfloat16)
    first = jnp.einsum("gab,nmtbc->nmgtac", tables, lowered, preferred_element_type=jnp.float32)
    middle = jnp.stack(
        [first[:, :, 0, 0] - first[:, :, 1, 1], first[:, :, 0, 1] + first[:, :, 1, 0]], axis=2
    ).astype(jnp.bfloat16)
    second = jnp.einsum("nmtab,gbc->nmtgac", middle, tables, preferred_element_type=jnp.float32)
    return jnp.stack(
        [second[:, :, 0, 0] - second[:, :, 1, 1], second[:, :, 0, 1] + second[:, :, 1, 0]], axis=2
    )


def propagate_many(values, table_re, table_im, kernel):
    return transform_many(
        times_complex(transform_many(values, table_re, table_im), kernel), table_re, -table_im
    )


def window_anchor(place):
    zero_index = jnp.int32(0)
    return (zero_index, zero_index, place[0], place[1])


def on_device(probe_modes, object_slices, amplitudes, scan_offsets, slot_counts):
    group = lax.axis_index("pos")
    tile_at = lax.axis_index("tile")
    strips = lax.axis_size("tile")
    slots = amplitudes.shape[0]
    points = amplitudes.shape[-1]
    layers = object_slices.shape[0]
    strip_rows = object_slices.shape[2]
    places = lax.dynamic_slice_in_dim(scan_offsets, group * slots, slots, 0)
    alive = (jnp.arange(slots, dtype=jnp.int32) < slot_counts[group]).astype(jnp.float32)
    padded = jnp.pad(object_slices, ((0, 0), (0, 0), (points, points), (0, 0)))

    def cut_piece(place):
        local_row = jnp.clip(place[0] - tile_at * strip_rows + points, 0, strip_rows + points)
        shifted_place = jnp.stack([local_row, place[1]])
        return lax.dynamic_slice(padded, window_anchor(shifted_place), (layers, 2, points, points))

    pieces = jax.vmap(cut_piece)(places).astype(jnp.float32)
    windows = lax.psum(pieces.astype(jnp.bfloat16), "tile").astype(jnp.float32)
    table_re, table_im, kernel = make_tables(points)
    kernel_conj = conjugate(kernel)
    current = times_complex(probe_modes[None], windows[:, None, 0])
    layer_at = 1
    arrived = propagate_many(current, table_re, table_im, kernel)
    entering = [arrived]
    current = times_complex(arrived, windows[:, None, layer_at])
    far_field = transform_many(current, table_re, table_im)
    partial_power = jnp.sum(far_field * far_field, axis=(1, 2))
    power = lax.psum(partial_power.astype(jnp.bfloat16), "tile").astype(jnp.float32)
    ratio = (1.0 - amplitudes.astype(jnp.float32) / jnp.sqrt(power + 1.0)) * alive[:, None, None]
    incoming = transform_many(ratio[:, None, None] * far_field, table_re, -table_im)
    object_terms = [None] * layers
    layer_at = 1
    object_terms[layer_at] = jnp.sum(
        times_complex(conjugate(entering[layer_at - 1]), incoming), axis=1
    )
    incoming = propagate_many(
        times_complex(conjugate(windows[:, None, layer_at]), incoming),
        table_re,
        table_im,
        kernel_conj,
    )
    object_terms[0] = jnp.sum(times_complex(conjugate(probe_modes[None]), incoming), axis=1)
    probe_term = jnp.sum(times_complex(conjugate(windows[:, None, 0]), incoming), axis=0)
    slot_grads = jnp.stack(object_terms, axis=1)
    canvas = jnp.zeros((layers, 2, strip_rows * strips, object_slices.shape[3]), jnp.float32)

    def deposit(canvas, packed):
        place, term = packed
        anchor = window_anchor(place)
        current_part = lax.dynamic_slice(canvas, anchor, term.shape)
        return (lax.dynamic_update_slice(canvas, current_part + term, anchor), None)

    canvas, unused = lax.scan(deposit, canvas, (places, slot_grads))
    column_part = lax.psum_scatter(
        canvas.astype(jnp.bfloat16), "pos", scatter_dimension=3, tiled=True
    )
    object_grad = lax.psum_scatter(column_part, "tile", scatter_dimension=2, tiled=True).astype(
        jnp.float32
    )
    probe_grad = lax.psum_scatter(
        probe_term.astype(jnp.bfloat16), "pos", scatter_dimension=2, tiled=True
    ).astype(jnp.float32)
    return (object_grad, probe_grad)


def solution(mesh):
    in_specs = (
        P("tile", None, None, None),
        P(None, None, "tile", None),
        P("pos", None, None),
        P(),
        P(),
    )
    out_specs = (P(None, None, "tile", "pos"), P("tile", None, "pos", None))
    return jax.shard_map(
        on_device, mesh=mesh, in_specs=in_specs, out_specs=out_specs, check_vma=False
    )
```

profile of v0, /device:TPU:0, one launch (start us, length us, event | category | flops | bytes accessed | tf_op | source)
XLA Modules:
  0.0 676.6 jit_solution(5778170829358070469)
XLA Ops:
  7.9 6.1 pad.4
  14.1 35.5 %while.12 = (s32[]{:T(128)}, bf16[2,2,576,2048]{3,2,1,0:T(8,128)(2,1)}, s32[8,4]{0,1:T(4,128)S(1)}, bf16[8,2,2,256,256]{3,4,0,2,1:T(8,128)(2,1)}, s32[]{:T(128)}) while((s32[]{:T(128)}, bf16[2,2,576,2048]{3,2,1,0:T(8,128)(2,1)}, s32[8,4]{0,1:T(4,128)S(1)}, bf16[8,2,2,256,256]{3,4,0,2,1:T(8,128)(2,1)}, s32[]{:T(128)}) %tuple.64), condition=%wide.while_cond, body=%wide.while_body.sunk | while | flops 2 | bytes 3145861 | solution.py:80
  14.7 2.6 dynamic-slice_bitcast_fusion.2
  19.1 2.7 dynamic-slice_bitcast_fusion.2
  23.5 2.7 dynamic-slice_bitcast_fusion.2
  28.0 2.7 dynamic-slice_bitcast_fusion.2
  32.4 2.7 dynamic-slice_bitcast_fusion.2
  36.9 2.7 dynamic-slice_bitcast_fusion.2
  41.3 2.7 dynamic-slice_bitcast_fusion.2
  45.8 2.7 dynamic-slice_bitcast_fusion.2
  53.0 1.9 fusion.87
  55.0 69.8 %all-reduce.6.cloned.1.call-done = bf16[8,2,2,256,256]{3,4,0,2,1:T(8,128)(2,1)} async-done(((bf16[8,2,2,256,256]{3,4,0,2,1:T(8,128)(2,1)}), bf16[8,2,2,256,256]{3,4,0,2,1:T(8,128)(2,1)}) %all-reduce.6.cloned.1.call-update) | async-done | bytes 4194320 | tf_op jit(solution)/shard_map/psum | solution.py:83
  124.8 3.2 convert_element_type.176
  136.2 2.7 fusion.52
  138.9 2.2 fusion.53
  143.0 1.5 convolution_bitcast_fusion.6
  144.5 1.8 fusion.71
  146.3 1.7 fusion.69
  148.0 1.5 fusion
  150.5 2.3 copy.98
  154.0 58.5 %all-reduce.8.cloned.1.call-done = bf16[8,256,256]{1,2,0:T(8,128)(2,1)} async-done(((bf16[8,256,256]{1,2,0:T(8,128)(2,1)}), bf16[8,256,256]{1,2,0:T(8,128)(2,1)}) %all-reduce.8.cloned.1.call-update) | async-done | bytes 1048592 | tf_op jit(solution)/shard_map/psum | solution.py:93
  212.5 2.2 subtract_multiply_fusion
  219.1 1.4 slice-done.1
  220.5 3.3 fusion.54
  223.7 6.3 multiply_subtract_fusion.1
  230.1 2.5 convolution_bitcast_fusion.3
  237.4 1.5 convolution_bitcast_fusion
  239.0 2.9 multiply_subtract_fusion
  241.9 4.0 multiply_subtract_fusion.2
  245.9 3.8 maximum_maximum_fusion
  249.7 7.9 %broadcast_in_dim.4 = f32[2,2,512,2048]{3,2,1,0:T(8,128)} broadcast(f32[]{:T(128)} %constant.34.clone.1), dimensions={} | broadcast | bytes 16777220 | tf_op jit(solution)/shard_map/broadcast_in_dim | solution.py:110
  257.6 154.4 %while.11 = (s32[]{:T(128)}, f32[2,2,512,2048]{3,2,1,0:T(8,128)}, s32[8,2]{0,1:T(2,128)S(1)}, f32[8,2,2,256,256]{3,4,0,2,1:T(8,128)}, s32[]{:T(128)}, /*index=5*/s32[]{:T(128)}, s32[]{:T(128)}, s32[]{:T(128)}) while((s32[]{:T(128)}, f32[2,2,512,2048]{3,2,1,0:T(8,128)}, s32[8,2]{0,1:T(2,128)S(1)}, f32[8,2,2,256,256]{3,4,0,2,1:T(8,128)}, ...), condition=%wide.region_4.5_spmd, body=%wide.region_3.4_spmd.sunk | while | flops 262152 | bytes 9437397 | solution.py:118
  261.9 1.3 constant_dynamic-slice_fusion.7
  263.6 1.6 bitcast_add_fusion.2
  265.2 8.4 %dynamic_update_slice.4 = f32[2,2,512,2048]{3,2,1,0:T(8,128)} dynamic-update-slice(f32[2,2,512,2048]{3,2,1,0:T(8,128)} %get-tuple-element.185, f32[2,2,256,256]{3,2,1,0:T(8,128)S(1)} %bitcast_add_fusion.2, s32[]{:T(128)} %constant.30.clone.1..sunk, s32[]{:T(128)} %constant.30.clone.1..sunk, s32[]{:T(128)S(6)} %select_n.106, s32[]{:T(128)S(6)} %select_n.107) | dynamic-update-slice | bytes 2097156 | tf_op jit(solution)/shard_map/while/body/eval_jaxpr/dynamic_update_slice | solution.py:116
  278.1 1.3 constant_dynamic-slice_fusion.7
  279.7 1.8 bitcast_add_fusion.2
  281.5 10.4 %dynamic_update_slice.4 = f32[2,2,512,2048]{3,2,1,0:T(8,128)} dynamic-update-slice(f32[2,2,512,2048]{3,2,1,0:T(8,128)} %get-tuple-element.185, f32[2,2,256,256]{3,2,1,0:T(8,128)S(1)} %bitcast_add_fusion.2, s32[]{:T(128)} %constant.30.clone.1..sunk, s32[]{:T(128)} %constant.30.clone.1..sunk, s32[]{:T(128)S(6)} %select_n.106, s32[]{:T(128)S(6)} %select_n.107) | dynamic-update-slice | bytes 2097156 | tf_op jit(solution)/shard_map/while/body/eval_jaxpr/dynamic_update_slice | solution.py:116
  296.3 1.3 constant_dynamic-slice_fusion.7
  298.0 1.8 bitcast_add_fusion.2
  299.8 12.3 %dynamic_update_slice.4 = f32[2,2,512,2048]{3,2,1,0:T(8,128)} dynamic-update-slice(f32[2,2,512,2048]{3,2,1,0:T(8,128)} %get-tuple-element.185, f32[2,2,256,256]{3,2,1,0:T(8,128)S(1)} %bitcast_add_fusion.2, s32[]{:T(128)} %constant.30.clone.1..sunk, s32[]{:T(128)} %constant.30.clone.1..sunk, s32[]{:T(128)S(6)} %select_n.106, s32[]{:T(128)S(6)} %select_n.107) | dynamic-update-slice | bytes 2097156 | tf_op jit(solution)/shard_map/while/body/eval_jaxpr/dynamic_update_slice | solution.py:116
  318.2 1.8 bitcast_add_fusion.2
  320.0 11.5 %dynamic_update_slice.4 = f32[2,2,512,2048]{3,2,1,0:T(8,128)} dynamic-update-slice(f32[2,2,512,2048]{3,2,1,0:T(8,128)} %get-tuple-element.185, f32[2,2,256,256]{3,2,1,0:T(8,128)S(1)} %bitcast_add_fusion.2, s32[]{:T(128)} %constant.30.clone.1..sunk, s32[]{:T(128)} %constant.30.clone.1..sunk, s32[]{:T(128)S(6)} %select_n.106, s32[]{:T(128)S(6)} %select_n.107) | dynamic-update-slice | bytes 2097156 | tf_op jit(solution)/shard_map/while/body/eval_jaxpr/dynamic_update_slice | solution.py:116
  337.6 1.8 bitcast_add_fusion.2
  339.4 12.3 %dynamic_update_slice.4 = f32[2,2,512,2048]{3,2,1,0:T(8,128)} dynamic-update-slice(f32[2,2,512,2048]{3,2,1,0:T(8,128)} %get-tuple-element.185, f32[2,2,256,256]{3,2,1,0:T(8,128)S(1)} %bitcast_add_fusion.2, s32[]{:T(128)} %constant.30.clone.1..sunk, s32[]{:T(128)} %constant.30.clone.1..sunk, s32[]{:T(128)S(6)} %select_n.106, s32[]{:T(128)S(6)} %select_n.107) | dynamic-update-slice | bytes 2097156 | tf_op jit(solution)/shard_map/while/body/eval_jaxpr/dynamic_update_slice | solution.py:116
  356.1 1.3 constant_dynamic-slice_fusion.7
  357.8 1.8 bitcast_add_fusion.2
  359.6 12.2 %dynamic_update_slice.4 = f32[2,2,512,2048]{3,2,1,0:T(8,128)} dynamic-update-slice(f32[2,2,512,2048]{3,2,1,0:T(8,128)} %get-tuple-element.185, f32[2,2,256,256]{3,2,1,0:T(8,128)S(1)} %bitcast_add_fusion.2, s32[]{:T(128)} %constant.30.clone.1..sunk, s32[]{:T(128)} %constant.30.clone.1..sunk, s32[]{:T(128)S(6)} %select_n.106, s32[]{:T(128)S(6)} %select_n.107) | dynamic-update-slice | bytes 2097156 | tf_op jit(solution)/shard_map/while/body/eval_jaxpr/dynamic_update_slice | solution.py:116
  376.2 1.3 constant_dynamic-slice_fusion.7
  377.8 1.8 bitcast_add_fusion.2
  379.7 12.4 %dynamic_update_slice.4 = f32[2,2,512,2048]{3,2,1,0:T(8,128)} dynamic-update-slice(f32[2,2,512,2048]{3,2,1,0:T(8,128)} %get-tuple-element.185, f32[2,2,256,256]{3,2,1,0:T(8,128)S(1)} %bitcast_add_fusion.2, s32[]{:T(128)} %constant.30.clone.1..sunk, s32[]{:T(128)} %constant.30.clone.1..sunk, s32[]{:T(128)S(6)} %select_n.106, s32[]{:T(128)S(6)} %select_n.107) | dynamic-update-slice | bytes 2097156 | tf_op jit(solution)/shard_map/while/body/eval_jaxpr/dynamic_update_slice | solution.py:116
  396.4 1.3 constant_dynamic-slice_fusion.7
  398.1 1.8 bitcast_add_fusion.2
  399.9 12.0 %dynamic_update_slice.4 = f32[2,2,512,2048]{3,2,1,0:T(8,128)} dynamic-update-slice(f32[2,2,512,2048]{3,2,1,0:T(8,128)} %get-tuple-element.185, f32[2,2,256,256]{3,2,1,0:T(8,128)S(1)} %bitcast_add_fusion.2, s32[]{:T(128)} %constant.30.clone.1..sunk, s32[]{:T(128)} %constant.30.clone.1..sunk, s32[]{:T(128)S(6)} %select_n.106, s32[]{:T(128)S(6)} %select_n.107) | dynamic-update-slice | bytes 2097156 | tf_op jit(solution)/shard_map/while/body/eval_jaxpr/dynamic_update_slice | solution.py:116
  411.9 9.1 %convert_element_type.183 = bf16[2,2,512,2048]{3,2,1,0:T(8,128)(2,1)} convert(f32[2,2,512,2048]{3,2,1,0:T(8,128)} %get-tuple-element.24) | non-fusion elementwise | flops 4194304 | bytes 25165824 | tf_op jit(solution)/shard_map/convert_element_type | solution.py:120
  421.1 21.3 %copy.200 = bf16[2,2,512,2048]{2,1,0,3:T(2,128)(2,1)} copy(bf16[2,2,512,2048]{3,2,1,0:T(8,128)(2,1)} %convert_element_type.183) | data formatting | bytes 16777216
  442.3 14.4 %reshape.1455 = bf16[2048,2048]{1,0:T(8,128)(2,1)} reshape(bf16[2048,2,2,512]{3,2,1,0:T(2,128)(2,1)} %bitcast.385) | data formatting | bytes 16777216
  456.9 1.5 copy-done.3
  458.4 1.9 maximum_reduce_fusion
  461.2 86.6 %reduce-scatter.7.cloned.1.call-done = bf16[128,2048]{1,0:T(8,128)(2,1)} async-done(((bf16[2048,2048]{1,0:T(8,128)(2,1)}), bf16[128,2048]{1,0:T(8,128)(2,1)}) %reduce-scatter.7.cloned.1.call-update) | async-done | bytes 524304
  547.9 1.4 reshape.1456
  551.7 83.5 %all-reduce.10.cloned.1.call-done = bf16[1,2,256,256]{3,1,0,2:T(2,128)(2,1)} async-done(((bf16[1,2,256,256]{3,1,0,2:T(2,128)(2,1)}), bf16[1,2,256,256]{3,1,0,2:T(2,128)(2,1)}) %all-reduce.10.cloned.1.call-update) | async-done | bytes 262160
  636.6 31.5 %reduce-scatter.5.cloned.1.call-done = bf16[2,2,64,128]{3,2,1,0:T(8,128)(2,1)} async-done(((bf16[2,2,512,128]{3,2,1,0:T(8,128)(2,1)}), bf16[2,2,64,128]{3,2,1,0:T(8,128)(2,1)}) %reduce-scatter.5.cloned.1.call-update) | async-done | bytes 65552 | tf_op jit(solution)/shard_map/reduce_scatter | solution.py:122
  668.1 1.5 convert_element_type.184
  (152 shorter events, 53.2 us)
Async XLA Ops:
  7.2 0.7 copy-start
  7.2 117.6 %all-reduce.6.cloned.1.call-start = ((), (), s32[]{:S(2)}) async-start(), calls=%async_computation.2 | async-start | bytes 8388608 | tf_op jit(solution)/shard_map/psum | solution.py:83
  49.6 1.0 copy-start.12
  49.6 162.9 %all-reduce.8.cloned.1.call-start = ((), (), s32[]{:S(2)}) async-start(), calls=%async_computation.3 | async-start | bytes 2097152 | tf_op jit(solution)/shard_map/psum | solution.py:93
  50.8 77.2 %copy-start.10 = (f32[256,256]{0,1:T(8,128)}, f32[256,256]{0,1:T(8,128)S(1)}, u32[]{:S(2)}) copy-start(f32[256,256]{0,1:T(8,128)S(1)} %copy.96) | copy-start | bytes 786436
  55.0 77.0 %copy-start.8 = (f32[256,256]{0,1:T(8,128)}, f32[256,256]{0,1:T(8,128)S(1)}, u32[]{:S(2)}) copy-start(f32[256,256]{0,1:T(8,128)S(1)} %get-tuple-element.98) | copy-start | bytes 786436
  128.0 10.8 %copy-start.2 = (f32[8,2,2,256,256]{3,4,0,2,1:T(8,128)}, f32[8,2,2,256,256]{3,4,0,2,1:T(8,128)S(1)}, u32[]{:S(2)}) copy-start(f32[8,2,2,256,256]{3,4,0,2,1:T(8,128)S(1)} %convert_element_type.176) | copy-start | bytes 25165828
  148.0 1.6 copy-start.13
  149.5 3.2 copy-start.16
  149.6 398.3 %reduce-scatter.7.cloned.1.call-start = ((), (), s32[]{:S(2)}) async-start(), calls=%async_computation.5 | async-start | bytes 8912896
  212.5 2.2 copy-start.4
  212.5 2.9 copy-start.5
  216.9 2.2 slice-start
  217.2 3.2 slice-start.1
  233.2 1.3 copy-start.9
  233.2 1.3 copy-start.14
  239.0 3.0 copy-start.11
  239.0 3.0 copy-start.15
  241.9 4.0 copy-start.6
  241.9 4.0 copy-start.7
  456.8 1.6 copy-start.3
  456.8 178.4 %all-reduce.10.cloned.1.call-start = ((), (), s32[]{:S(2)}) async-start(), calls=%async_computation.6 | async-start | bytes 524288
  458.4 211.2 %copy-start.1 = (s32[128,2]{0,1:T(2,128)S(1)}, s32[128,2]{0,1:T(2,128)}, u32[]{:S(2)}) copy-start(s32[128,2]{0,1:T(2,128)} %param.10) | copy-start | bytes 3076
  460.3 90.2 %copy-start.17 = (u32[128]{0:T(128)S(1)}, u32[128]{0:T(128)}, u32[]{:S(2)}) copy-start(u32[128]{0:T(128)} %constant.103) | copy-start | bytes 1540
  461.2 206.9 %reduce-scatter.5.cloned.1.call-start = ((), (), s32[]{:S(2)}) async-start(), calls=%async_computation.4 | async-start | bytes 589824 | tf_op jit(solution)/shard_map/reduce_scatter | solution.py:122
Sparse Core Ops, SparseCore 0:
  49.7 75.0 all-reduce.5
  149.7 62.7 all-reduce.7
  456.9 90.8 reduce-scatter.6
  550.9 84.3 all-reduce.9
  637.5 30.5 reduce-scatter.4
where the time goes:
time: 689 us; the launch traced here: 677 us
  waiting for transfers between devices  330 us (48%)
  local copies, waits for them, and re-layouts  209 us (30%)
  other arithmetic  74.4 us (11%)
  loops' own time  30.6 us (4%)
  matrix products  17.1 us (2%)
  between operations  15.3 us (2%)
    unnamed x7, waiting for transfers between devices  170 us
    dynamic_update_slice x8, local copies, waits for them, and re-layouts, deposit(): return (lax.dynamic_update_slice(canvas, current_part + term, anchor), None)  91.6 us
    psum x1, waiting for transfers between devices, on_device(): windows = lax.psum(pieces.astype(jnp.bfloat16), 'tile').astype(jnp.float32)  69.8 us
    psum x1, waiting for transfers between devices, on_device(): lax.psum(partial_power.astype(jnp.bfloat16), 'tile').astype(jnp.float32)  58.5 us
    unnamed x47, local copies, waits for them, and re-layouts  47.5 us
    gather x40, local copies, waits for them, and re-layouts  35.4 us
    reduce_scatter x1, waiting for transfers between devices, on_device(): lax.psum_scatter(column_part, 'tile', scatter_dimension=2, tiled=True)  31.5 us
    another operation x1, loops' own time, on_device(): canvas, unused = lax.scan(deposit, canvas, (places, slot_grads))  30.5 us
  transfers between devices with their start and end apart: 5, of which 5 were waited for; matrix products, arithmetic and copies ran while one was open for 2% of the time, Pallas kernels for 0%

commit v1 on v0

v1 whole, which is shorter than its diff:
```python
import functools

import jax
import jax.numpy as jnp
import numpy as np
from jax import lax
from jax.experimental import pallas as pl
from jax.experimental.pallas import tpu as pltpu
from jax.sharding import PartitionSpec as P

FRESNEL = 0.37
LINE = 4
F32 = jnp.float32
BF16 = jnp.bfloat16
MESH = pl.DeviceIdType.MESH


def tables(points):
    counter = np.arange(points, dtype=np.int32)
    product = counter[:, None] * counter[None, :] % points
    angle = np.float32(2.0 * np.pi / points) * product.astype(np.float32)
    factor = np.float32(1.0) / np.sqrt(np.float32(points))
    re = (np.cos(angle) * factor).astype(np.float32)
    im = (-np.sin(angle) * factor).astype(np.float32)
    a = np.block([[re, -im], [im, re]]).astype(jnp.bfloat16)
    b = np.block([[re, im], [-im, re]]).astype(jnp.bfloat16)
    shifted = ((counter + points // 2) % points - points // 2).astype(np.float32)
    phase = np.float32(np.pi * FRESNEL / points) * (shifted[:, None] ** 2 + shifted[None, :] ** 2)
    ker = np.stack([np.cos(phase), -np.sin(phase)]).astype(np.float32)
    return a, b, ker


def one_hot(shape, shift, transposed=False):
    rows = lax.broadcasted_iota(jnp.int32, shape, 0)
    cols = lax.broadcasted_iota(jnp.int32, shape, 1)
    hit = (cols == rows + shift) if transposed else (rows == cols + shift)
    return jnp.where(hit, 1.0, 0.0).astype(BF16)


def dot(left, right):
    return jnp.dot(left, right, preferred_element_type=F32)


def body(
    counts, offs, probe, strip, amp, amat, bmat, ker, obj_out, prb_out,
    tall, wsend, wbuf, win, prb, asend, arecv, ahalf, phi, far, pwsend, pwrecv, ratio, xin,
    g1, g0, sibs, sibr, own, gys, gyr, pad, canvas, posr, gps, gpr, gsum, gfr,
    w_ss, w_rs, rl_ss, rl_rs, p_ss, p_rs, a_ss, a_rs, ah_ss, ah_rs, pw_ss, pw_rs,
    sb_ss, sb_rs, gy_ss, gy_rs, ps_ss, ps_rs, gp_ss, gp_rs, gf_ss, gf_rs,
    *, n_pos,
):
    p = lax.axis_index("pos")
    t = lax.axis_index("tile")
    y = lax.div(t, 2)
    c = lax.rem(t, 2)
    S = ker.shape[1]
    H = S // 2
    layers, _, SR, C = strip.shape
    CW = C // n_pos
    slots = amp.shape[0]
    groups = counts.shape[0]
    RW = SR * 2 * LINE

    def at_y(i):
        return lax.rem(y + i, LINE)

    def ydev(i):
        return (p, 2 * at_y(i) + c)

    sib = (p, 2 * y + 1 - c)

    def pdev(d):
        return (lax.rem(p + d, n_pos), t)

    def copy(src, dst, ss, rs, dev):
        return pltpu.make_async_remote_copy(
            src_ref=src, dst_ref=dst, send_sem=ss, recv_sem=rs, device_id=dev, device_id_type=MESH
        )

    barrier = pltpu.get_barrier_semaphore()
    partners = [ydev(i) for i in range(1, LINE)] + [sib] + [pdev(d) for d in range(1, n_pos)]
    for dev in partners:
        pl.semaphore_signal(barrier, inc=1, device_id=dev, device_id_type=MESH)

    def locate(k):
        g = jnp.int32(0)
        start = jnp.int32(0)
        end = jnp.int32(0)
        for q in range(groups):
            end = end + counts[q]
            past = end <= k
            g = jnp.where(past, q + 1, g)
            start = jnp.where(past, end, start)
        return jnp.clip(slots * g + (k - start), 0, slots * groups - 1)

    row_of, base_of, shift_of = [], [], []
    for i in range(LINE):
        s = locate(LINE * p + at_y(i))
        row_of.append(offs[s, 0])
        col = offs[s, 1]
        block = jnp.int32(0)
        for q in range(1, (C - S) // 128):
            block = jnp.where(col >= q * 128, q, block)
        base_of.append(block)
        shift_of.append(col - block * 128)
    wide = S + 128
    my_row = row_of[0]

    my_start = jnp.int32(0)
    for q in range(groups):
        my_start = my_start + jnp.where(q < p, counts[q], 0)
    my_count = counts[p]

    def crop(l):
        for q in range(C // 128):
            tall[l, q] = strip[l, :, :, q * 128 : (q + 1) * 128].reshape(2 * SR, 128)
        for i in range(LINE):
            sel = one_hot((wide, S), shift_of[i])
            blk = jnp.concatenate([tall[l, base_of[i] + q] for q in range(wide // 128)], axis=-1)
            out = dot(blk, sel).astype(BF16).reshape(2, SR, S)
            if i == 0:
                wbuf[l, :, pl.ds(pl.multiple_of(t * SR, SR), SR), :] = out
            else:
                wsend[l, i] = out

    def strip_rows(i):
        return pl.ds(pl.multiple_of((2 * at_y(i) + c) * SR, SR), SR)

    def w_copy(l, i):
        mine = pl.ds(pl.multiple_of(t * SR, SR), SR)
        return copy(wsend.at[l, i], wbuf.at[l, :, mine, :], w_ss.at[l, i], w_rs.at[l, i], ydev(i))

    def relay(l, i):
        ref = wbuf.at[l, :, strip_rows(LINE - i), :]
        return copy(ref, ref, rl_ss.at[l, i], rl_rs.at[l, i], sib)

    def p_copy(i):
        return copy(prb.at[0], prb.at[i], p_ss.at[i], p_rs.at[i], ydev(LINE - i))

    def a_copy(d):
        return copy(asend.at[d], arecv.at[d], a_ss.at[d], a_rs.at[d], pdev(d))

    near = (1, 3, 2)
    prb[0] = probe[0].astype(BF16)
    crop(0)
    pl.semaphore_wait(barrier, len(partners))
    for i in near:
        w_copy(0, i).start()
    relay(0, 0).start()
    for i in near:
        p_copy(i).start()
    crop(1)
    for i in near:
        w_copy(1, i).start()
    relay(1, 0).start()

    rows_c = pl.ds(pl.multiple_of(c * H, H), H)
    for d in range(n_pos):
        j = LINE * lax.rem(p + d, n_pos) + y - my_start
        keep = jnp.where((j >= 0) & (j < my_count), 1.0, 0.0)
        block = amp[jnp.clip(j, 0, slots - 1), rows_c, :].astype(F32) * keep
        if d == 0:
            arecv[0] = block.astype(BF16)
        else:
            asend[d] = block.astype(BF16)
    for d in range(1, n_pos):
        a_copy(d).start()

    def gather(l):
        for i in near:
            w_copy(l, i).wait_recv()
            relay(l, i).start()
        for i in range(LINE):
            relay(l, i).wait_recv()
        sel = one_hot((S, RW), my_row, transposed=True)
        win[l, 0] = dot(sel, wbuf[l, 0])
        win[l, 1] = dot(sel, wbuf[l, 1])

    def transform(re, im, left, right):
        x = jnp.concatenate([re.astype(BF16), im.astype(BF16)], axis=0)
        return transform_low(x, left, right)

    def transform_low(x, left, right):
        mid = dot(left[...], x).astype(BF16)
        out = dot(jnp.concatenate([mid[:S], mid[S:]], axis=1), right[...])
        return out[:, :S], out[:, S:]

    def forward_a(i):
        pr, pi = prb[i, 0].astype(F32), prb[i, 1].astype(F32)
        wr, wi = win[0, 0], win[0, 1]
        fr, fi = transform(pr * wr - pi * wi, pr * wi + pi * wr, amat, bmat)
        kr, ki = ker[0], ker[1]
        fr, fi = transform(fr * kr - fi * ki, fr * ki + fi * kr, bmat, amat)
        phi[i, 0] = fr
        phi[i, 1] = fi

    def forward_b(i):
        pr, pi = phi[i, 0], phi[i, 1]
        wr, wi = win[1, 0], win[1, 1]
        fr, fi = transform(pr * wr - pi * wi, pr * wi + pi * wr, amat, bmat)
        far[i, 0] = fr
        far[i, 1] = fi
        return fr * fr + fi * fi

    gather(0)
    forward_a(0)
    gather(1)
    ratio[...] = forward_b(0)
    for i in near:
        p_copy(i).wait_recv()
        forward_a(i)
        ratio[...] = ratio[...] + forward_b(i)

    pw_c = copy(pwsend, pwrecv, pw_ss.at[0], pw_rs.at[0], sib)
    pwsend[...] = ratio[...].astype(BF16)
    pw_c.start()
    total = arecv[0].astype(F32)
    for d in range(1, n_pos):
        a_copy(d).wait_recv()
        total = total + arecv[d].astype(F32)
    ahalf[rows_c, :] = total.astype(BF16)
    ah_c = copy(ahalf.at[rows_c, :], ahalf.at[rows_c, :], ah_ss.at[0], ah_rs.at[0], sib)
    ah_c.start()
    pw_c.wait_recv()
    power = ratio[...] + pwrecv[...].astype(F32)
    ah_c.wait_recv()
    ratio[...] = 1.0 - ahalf[...].astype(F32) / jnp.sqrt(power + 1.0)

    def backward_a(i, first):
        r = ratio[...]
        br, bi = transform(r * far[i, 0], r * far[i, 1], bmat, amat)
        pr, pi = phi[i, 0], phi[i, 1]
        gr = pr * br + pi * bi
        gi = pr * bi - pi * br
        if first:
            g1[0] = gr
            g1[1] = gi
        else:
            g1[0] = g1[0] + gr
            g1[1] = g1[1] + gi
        wr, wi = win[1, 0], win[1, 1]
        xin[i, :S] = (wr * br + wi * bi).astype(BF16)
        xin[i, S:] = (wr * bi - wi * br).astype(BF16)

    def backward_b(i, first):
        fr, fi = transform_low(xin[i], amat, bmat)
        kr, ki = ker[0], ker[1]
        br, bi = transform(fr * kr + fi * ki, fi * kr - fr * ki, bmat, amat)
        pr, pi = prb[i, 0].astype(F32), prb[i, 1].astype(F32)
        gr = pr * br + pi * bi
        gi = pr * bi - pi * br
        if first:
            g0[0] = gr
            g0[1] = gi
        else:
            g0[0] = g0[0] + gr
            g0[1] = g0[1] + gi
        wr, wi = win[0, 0], win[0, 1]
        gps[i, 0] = (wr * br + wi * bi).astype(BF16)
        gps[i, 1] = (wr * bi - wi * br).astype(BF16)

    def sb_copy(l):
        return copy(sibs.at[l], sibr.at[l], sb_ss.at[l], sb_rs.at[l], sib)

    def gy_copy(l, i):
        return copy(gys.at[l, i], gyr.at[l, i], gy_ss.at[l, i], gy_rs.at[l, i], ydev(i))

    def ps_copy(l, d):
        return copy(canvas.at[l, lax.rem(p + d, n_pos)], posr.at[l, d], ps_ss.at[l, d], ps_rs.at[l, d], pdev(d))

    def place_rows(l, grad):
        rows = lax.broadcasted_iota(jnp.int32, (RW, S), 0)
        cols = lax.broadcasted_iota(jnp.int32, (RW, S), 1)
        block = rows // SR
        strip_at = 2 * ((y + block % LINE) % LINE) + jnp.where(block < LINE, c, 1 - c)
        hit = strip_at * SR + rows % SR == cols + my_row
        sel = jnp.where(hit, 1.0, 0.0).astype(BF16)
        for part in range(2):
            out = dot(sel, grad[part].astype(BF16)).astype(BF16)
            for i in range(LINE):
                own[l, i, part] = out[i * SR : (i + 1) * SR]
                sibs[l, i, part] = out[(LINE + i) * SR : (LINE + i + 1) * SR]
        sb_copy(l).start()

    def add_cores(l):
        sb_copy(l).wait_recv()
        for i in (0, 2, 1, 3):
            both = (own[l, i].astype(F32) + sibr[l, i].astype(F32)).astype(BF16)
            if i == 0:
                gyr[l, 0] = both
            else:
                gys[l, i] = both
                gy_copy(l, i).start()

    def place_columns(l):
        for i in range(LINE):
            if i:
                gy_copy(l, i).wait_recv()
            k = (LINE - i) % LINE
            sel = one_hot((S, wide), shift_of[k], transposed=True)
            out = dot(gyr[l, i].reshape(2 * SR, S), sel).astype(BF16)
            for q in range(wide // 128):
                pad[l, i, q + 1] = out[:, q * 128 : (q + 1) * 128].reshape(2, SR, 128)
        per = CW // 128
        for q in range(C // 128):
            total = None
            for i in range(LINE):
                k = (LINE - i) % LINE
                at = jnp.clip(q - base_of[k], -1, wide // 128) + 1
                term = pad[l, i, at].astype(F32)
                total = term if total is None else total + term
            canvas[l, q // per, :, :, (q % per) * 128 : (q % per + 1) * 128] = total.astype(BF16)
        for d in range(1, n_pos):
            ps_copy(l, d).start()

    def finish(l):
        total = canvas[l, p].astype(F32)
        for d in range(1, n_pos):
            ps_copy(l, d).wait_recv()
            total = total + posr[l, d].astype(F32)
        obj_out[l] = total

    def gp_copy(i):
        return copy(gps.at[i], gpr.at[i], gp_ss.at[i], gp_rs.at[i], ydev(i))

    PR = S // n_pos

    def gf_copy(d):
        rows = pl.ds(pl.multiple_of(lax.rem(p + d, n_pos) * PR, PR), PR)
        return copy(gsum.at[:, rows, :], gfr.at[d], gf_ss.at[d], gf_rs.at[d], pdev(d))

    for n, i in enumerate((2, 1, 3, 0)):
        backward_a(i, n == 0)
    place_rows(1, g1)
    for l in range(layers):
        for i in range(LINE):
            pad[l, i, 0] = jnp.zeros((2, SR, 128), BF16)
            pad[l, i, wide // 128 + 1] = jnp.zeros((2, SR, 128), BF16)
    for n, i in enumerate((2, 1, 3, 0)):
        backward_b(i, n == 0)
        if i:
            gp_copy(i).start()
        if n == 0:
            add_cores(1)
        if n == 2:
            place_columns(1)
    place_rows(0, g0)
    gp_copy(1).wait_recv()
    gp_copy(3).wait_recv()
    gp_copy(2).wait_recv()
    for part in range(2):
        total = gps[0, part].astype(F32)
        for i in range(1, LINE):
            total = total + gpr[i, part].astype(F32)
        gsum[part] = total.astype(BF16)
    for d in range(1, n_pos):
        gf_copy(d).start()
    add_cores(0)
    place_columns(0)
    finish(1)
    my_rows = pl.ds(pl.multiple_of(p * PR, PR), PR)
    total = gsum[:, my_rows, :].astype(F32)
    for d in range(1, n_pos):
        gf_copy(d).wait_recv()
        total = total + gfr[d].astype(F32)
    prb_out[0] = total
    finish(0)

    for i in range(1, LINE):
        p_copy(i).wait_send()
        gp_copy(i).wait_send()
        for l in range(layers):
            w_copy(l, i).wait_send()
            gy_copy(l, i).wait_send()
    for l in range(layers):
        sb_copy(l).wait_send()
        for i in range(LINE):
            relay(l, i).wait_send()
        for d in range(1, n_pos):
            ps_copy(l, d).wait_send()
    for d in range(1, n_pos):
        a_copy(d).wait_send()
        gf_copy(d).wait_send()
    pw_c.wait_send()
    ah_c.wait_send()


def on_device(n_pos, consts, probe_modes, object_slices, amplitudes, scan_offsets, slot_counts):
    S = probe_modes.shape[-1]
    layers, _, SR, C = object_slices.shape
    CW = C // n_pos
    RW = SR * 2 * LINE
    wide = S + 128
    vm = pltpu.VMEM
    dma = pltpu.SemaphoreType.DMA
    scratch = [
        vm((layers, C // 128, 2 * SR, 128), BF16),
        vm((layers, LINE, 2, SR, S), BF16),
        vm((layers, 2, RW, S), BF16),
        vm((layers, 2, S, S), F32),
        vm((LINE, 2, S, S), BF16),
        vm((n_pos, S // 2, S), BF16),
        vm((n_pos, S // 2, S), BF16),
        vm((S, S), BF16),
        vm((LINE, 2, S, S), F32),
        vm((LINE, 2, S, S), F32),
        vm((S, S), BF16),
        vm((S, S), BF16),
        vm((S, S), F32),
        vm((LINE, 2 * S, S), BF16),
        vm((2, S, S), F32),
        vm((2, S, S), F32),
        vm((layers, LINE, 2, SR, S), BF16),
        vm((layers, LINE, 2, SR, S), BF16),
        vm((layers, LINE, 2, SR, S), BF16),
        vm((layers, LINE, 2, SR, S), BF16),
        vm((layers, LINE, 2, SR, S), BF16),
        vm((layers, LINE, wide // 128 + 2, 2, SR, 128), BF16),
        vm((layers, n_pos, 2, SR, CW), BF16),
        vm((layers, n_pos, 2, SR, CW), BF16),
        vm((LINE, 2, S, S), BF16),
        vm((LINE, 2, S, S), BF16),
        vm((2, S, S), BF16),
        vm((n_pos, 2, S // n_pos, S), BF16),
    ]
    for shape in (
        (layers, LINE), (layers, LINE), (LINE,), (n_pos,), (1,), (1,),
        (layers,), (layers, LINE), (layers, n_pos), (LINE,), (n_pos,),
    ):
        scratch += [dma(shape), dma(shape)]
    smem = pl.BlockSpec(memory_space=pltpu.SMEM)
    vmem = pl.BlockSpec(memory_space=pltpu.VMEM)
    return pl.pallas_call(
        functools.partial(body, n_pos=n_pos),
        out_shape=(
            jax.ShapeDtypeStruct((layers, 2, SR, CW), F32),
            jax.ShapeDtypeStruct((1, 2, S // n_pos, S), F32),
        ),
        in_specs=[smem, smem] + [vmem] * 6,
        out_specs=(vmem, vmem),
        scratch_shapes=scratch,
        compiler_params=pltpu.CompilerParams(
            collective_id=0, has_side_effects=True, vmem_limit_bytes=60 * 1024 * 1024
        ),
        name="ptycho",
    )(slot_counts, scan_offsets, probe_modes, object_slices, amplitudes, *consts)


def solution(mesh):
    n_pos = mesh.shape["pos"]
    in_specs = (
        P("tile", None, None, None),
        P(None, None, "tile", None),
        P("pos", None, None),
        P(),
        P(),
    )
    out_specs = (P(None, None, "tile", "pos"), P("tile", None, "pos", None))

    def run(probe_modes, object_slices, amplitudes, scan_offsets, slot_counts):
        consts = tuple(jnp.asarray(v) for v in tables(probe_modes.shape[-1]))
        return jax.shard_map(
            lambda *args: on_device(n_pos, args[5:], *args[:5]),
            mesh=mesh,
            in_specs=in_specs + (P(), P(), P()),
            out_specs=out_specs,
            check_vma=False,
        )(probe_modes, object_slices, amplitudes, scan_offsets, slot_counts, *consts)

    return run
```

time: 689 us -> 78.9 us (0.11); the launches traced: 677 us -> 78.7 us
  waiting for transfers between devices: 330 us -> 0 us
  local copies, waits for them, and re-layouts: 209 us -> 3.61 us
  Pallas kernels: 0 us -> 74.5 us
  other arithmetic: 74.4 us -> 0 us
  loops' own time: 30.6 us -> 0 us
  matrix products: 17.1 us -> 0 us
  between operations: 15.3 us -> 0.65 us
    unnamed x7 -> x0, waiting for transfers between devices: 170 us -> none
    psum x2 -> x0, waiting for transfers between devices: 128 us -> none  [the longest x1 69.8 us: on_device(): windows = lax.psum(pieces.astype(jnp.bfloat16), 'tile').astype(jnp.float32)]
    dynamic_update_slice x8 -> x0, local copies, waits for them, and re-layouts: 91.6 us -> none  [deposit(): return (lax.dynamic_update_slice(canvas, current_part + term, anchor), None)]
    pallas_call x0 -> x1, Pallas kernels: none -> 74.5 us  [on_device(): pl.pallas_call(functools.partial(body, n_pos=n_pos), out_shape=(jax.Shape...]
    unnamed x47 -> x5, local copies, waits for them, and re-layouts: 47.5 us -> 3.61 us
    gather x40 -> x0, local copies, waits for them, and re-layouts: 35.4 us -> none
    reduce_scatter x1 -> x0, waiting for transfers between devices: 31.5 us -> none  [on_device(): lax.psum_scatter(column_part, 'tile', scatter_dimension=2, tiled=True)]
    another operation x2 -> x0, loops' own time: 30.6 us -> none  [the longest x1 30.5 us: on_device(): canvas, unused = lax.scan(deposit, canvas, (places, slot_grads))]
  transfers between devices with their start and end apart: 5 -> 0, of which waited for: 5 -> 0; matrix products, arithmetic and copies ran while one was open for 2% -> 0% of each run, Pallas kernels for 0% -> 0%
where the time goes in v1:
time: 78.9 us; the launch traced here: 78.7 us
  Pallas kernels  74.5 us (94%)
  local copies, waits for them, and re-layouts  3.61 us (5%)
    pallas_call x1, Pallas kernels, on_device(): pl.pallas_call(functools.partial(body, n_pos=n_pos), out_shape=(jax.Shape...  74.5 us
    unnamed x5, local copies, waits for them, and re-layouts  3.61 us

profile of v1, /device:TPU:0, one launch (start us, length us, event | category | flops | bytes accessed | tf_op | source)
XLA Modules:
  0.0 78.7 jit_solution(1525286721147636534)
XLA Ops:
  0.6 1.4 %copy.10.offs = s32[128,2]{1,0:T(8,128)} copy(s32[128,2]{0,1:T(2,128)} %param.11) | data formatting | bytes 2048 | tf_op args[3]
  2.0 74.5 %ptycho.1 = (f32[2,2,64,128]{3,2,1,0:T(8,128)}, f32[1,2,16,256]{3,2,1,0:T(8,128)}) custom-call(s32[16]{0:T(128)} %counts.1, s32[128,2]{1,0:T(8,128)} %copy.10.offs, f32[1,2,256,256]{3,2,1,0:T(8,128)} %probe.1, bf16[2,2,64,2048]{3,2,1,0:T(8,128)(2,1)} %strip.1, bf16[8,256,256]{2,1,0:T(8,128)(2,1)} %amp.1, bf16[512,512]{1,0:T(8,128)(2,1)} %constant.6.clone.amat, ...), custom_call_target="tpu_custom_call" | custom-call | tf_op jit(solution)/shard_map/ptycho/pallas_call | solution.py:433
  76.5 0.0 copy-start
  76.5 1.6 %copy.13 = f32[2,2,64,128]{3,2,1,0:T(8,128)} copy(f32[2,2,64,128]{3,2,1,0:T(8,128)} %get-tuple-element.4) | data formatting | bytes 262144
  78.1 0.0 copy-done
  78.1 0.6 copy.14
Async XLA Ops:
  76.5 1.6 %copy-start = (f32[1,2,16,256]{3,2,1,0:T(8,128)S(1)}, f32[1,2,16,256]{3,2,1,0:T(8,128)}, u32[]{:S(2)}) copy-start(f32[1,2,16,256]{3,2,1,0:T(8,128)} %get-tuple-element.5) | copy-start | bytes 98308

commit v2 on v1

--- a/solution.py
+++ b/solution.py
@@ -1,4 +1,5 @@
 import functools
+import math
 
 import jax
 import jax.numpy as jnp
@@ -42,11 +43,12 @@
 
 
 def body(
-    counts, offs, probe, strip, amp, amat, bmat, ker, obj_out, prb_out,
+    counts, offs, probe_in, strip_in, amp_in, amat_in, bmat_in, ker_in, obj_out, prb_out,
+    probe, strip, amp, amat, bmat, ker,
     tall, wsend, wbuf, win, prb, asend, arecv, ahalf, phi, far, pwsend, pwrecv, ratio, xin,
-    g1, g0, sibs, sibr, own, gys, gyr, pad, canvas, posr, gps, gpr, gsum, gfr,
+    g1, g0, sibs, sibr, own, gys, gyr, pad, canvas, posr, gps, h1, h, h2, k2, k3, load,
     w_ss, w_rs, rl_ss, rl_rs, p_ss, p_rs, a_ss, a_rs, ah_ss, ah_rs, pw_ss, pw_rs,
-    sb_ss, sb_rs, gy_ss, gy_rs, ps_ss, ps_rs, gp_ss, gp_rs, gf_ss, gf_rs,
+    sb_ss, sb_rs, gy_ss, gy_rs, ps_ss, ps_rs, f1_ss, f1_rs, f2_ss, f2_rs, f3_ss, f3_rs,
     *, n_pos,
 ):
     p = lax.axis_index("pos")
@@ -60,6 +62,15 @@
     slots = amp.shape[0]
     groups = counts.shape[0]
     RW = SR * 2 * LINE
+    PR = S // n_pos
+    N = math.isqrt(n_pos)
+    at_axis = (lax.div(p, N), lax.rem(p, N))
+
+    def axis_dev(n, d):
+        x, z = at_axis
+        if n == 0:
+            return (lax.rem(x + d, N) * N + z, t)
+        return (x * N + lax.rem(z + d, N), t)
 
     def at_y(i):
         return lax.rem(y + i, LINE)
@@ -76,6 +87,12 @@
         return pltpu.make_async_remote_copy(
             src_ref=src, dst_ref=dst, send_sem=ss, recv_sem=rs, device_id=dev, device_id_type=MESH
         )
+
+    ins = (strip_in, probe_in, amp_in, amat_in, bmat_in, ker_in)
+    held = (strip, probe, amp, amat, bmat, ker)
+    loads = [pltpu.make_async_copy(ins[n], held[n], load.at[n]) for n in range(len(ins))]
+    for one in loads:
+        one.start()
 
     barrier = pltpu.get_barrier_semaphore()
     partners = [ydev(i) for i in range(1, LINE)] + [sib] + [pdev(d) for d in range(1, n_pos)]
@@ -96,8 +113,8 @@
     row_of, base_of, shift_of = [], [], []
     for i in range(LINE):
         s = locate(LINE * p + at_y(i))
-        row_of.append(offs[s, 0])
-        col = offs[s, 1]
+        row_of.append(offs[0, s])
+        col = offs[1, s]
         block = jnp.int32(0)
         for q in range(1, (C - S) // 128):
             block = jnp.where(col >= q * 128, q, block)
@@ -137,23 +154,30 @@
     def p_copy(i):
         return copy(prb.at[0], prb.at[i], p_ss.at[i], p_rs.at[i], ydev(LINE - i))
 
+    def p_pass(n):
+        i = (1, 3)[n]
+        return copy(prb.at[i, n], prb.at[2, n], p_ss.at[2 * n], p_rs.at[2 * n], ydev(LINE - i))
+
     def a_copy(d):
         return copy(asend.at[d], arecv.at[d], a_ss.at[d], a_rs.at[d], pdev(d))
 
     near = (1, 3, 2)
+    loads[0].wait()
+    crop(0)
+    loads[1].wait()
     prb[0] = probe[0].astype(BF16)
-    crop(0)
     pl.semaphore_wait(barrier, len(partners))
     for i in near:
         w_copy(0, i).start()
     relay(0, 0).start()
-    for i in near:
-        p_copy(i).start()
     crop(1)
     for i in near:
         w_copy(1, i).start()
+    for i in (1, 3):
+        p_copy(i).start()
     relay(1, 0).start()
 
+    loads[2].wait()
     rows_c = pl.ds(pl.multiple_of(c * H, H), H)
     for d in range(n_pos):
         j = LINE * lax.rem(p + d, n_pos) + y - my_start
@@ -202,12 +226,24 @@
         far[i, 1] = fi
         return fr * fr + fi * fi
 
+    for l in range(layers):
+        for i in range(LINE):
+            for part in range(2):
+                pad[l, part, i, 0] = jnp.zeros((SR, 128), BF16)
+                pad[l, part, i, wide // 128 + 1] = jnp.zeros((SR, 128), BF16)
     gather(0)
+    for n in (3, 4, 5):
+        loads[n].wait()
     forward_a(0)
     gather(1)
     ratio[...] = forward_b(0)
+    for n in range(2):
+        p_copy((1, 3)[n]).wait_recv()
+        p_pass(n).start()
     for i in near:
-        p_copy(i).wait_recv()
+        if i == 2:
+            p_pass(0).wait_recv()
+            p_pass(1).wait_recv()
         forward_a(i)
         ratio[...] = ratio[...] + forward_b(i)
 
@@ -256,17 +292,23 @@
             g0[0] = g0[0] + gr
             g0[1] = g0[1] + gi
         wr, wi = win[0, 0], win[0, 1]
-        gps[i, 0] = (wr * br + wi * bi).astype(BF16)
-        gps[i, 1] = (wr * bi - wi * br).astype(BF16)
-
-    def sb_copy(l):
-        return copy(sibs.at[l], sibr.at[l], sb_ss.at[l], sb_rs.at[l], sib)
-
-    def gy_copy(l, i):
-        return copy(gys.at[l, i], gyr.at[l, i], gy_ss.at[l, i], gy_rs.at[l, i], ydev(i))
-
-    def ps_copy(l, d):
-        return copy(canvas.at[l, lax.rem(p + d, n_pos)], posr.at[l, d], ps_ss.at[l, d], ps_rs.at[l, d], pdev(d))
+        pr = (wr * br + wi * bi).astype(BF16)
+        pi = (wr * bi - wi * br).astype(BF16)
+        for a in range(N):
+            for b in range(N):
+                rows = slice((a * N + b) * PR, (a * N + b + 1) * PR)
+                gps[i, 0, a, b] = pr[rows]
+                gps[i, 1, b, a] = pi[rows]
+
+    def sb_copy(l, m):
+        return copy(sibs.at[l, m], sibr.at[l, m], sb_ss.at[l, m], sb_rs.at[l, m], sib)
+
+    def gy_copy(l, m, i):
+        return copy(gys.at[l, m, i], gyr.at[l, m, i], gy_ss.at[l, m, i], gy_rs.at[l, m, i], ydev(i))
+
+    def ps_copy(l, m, d):
+        src = canvas.at[l, m, lax.rem(p + d, n_pos)]
+        return copy(src, posr.at[l, m, d], ps_ss.at[l, m, d], ps_rs.at[l, m, d], pdev(d))
 
     def place_rows(l, grad):
         rows = lax.broadcasted_iota(jnp.int32, (RW, S), 0)
@@ -275,112 +317,139 @@
         strip_at = 2 * ((y + block % LINE) % LINE) + jnp.where(block < LINE, c, 1 - c)
         hit = strip_at * SR + rows % SR == cols + my_row
         sel = jnp.where(hit, 1.0, 0.0).astype(BF16)
-        for part in range(2):
-            out = dot(sel, grad[part].astype(BF16)).astype(BF16)
+        for m in range(2):
+            out = dot(sel, grad[m].astype(BF16)).astype(BF16)
             for i in range(LINE):
-                own[l, i, part] = out[i * SR : (i + 1) * SR]
-                sibs[l, i, part] = out[(LINE + i) * SR : (LINE + i + 1) * SR]
-        sb_copy(l).start()
-
-    def add_cores(l):
-        sb_copy(l).wait_recv()
-        for i in (0, 2, 1, 3):
-            both = (own[l, i].astype(F32) + sibr[l, i].astype(F32)).astype(BF16)
+                own[l, m, i] = out[i * SR : (i + 1) * SR]
+                sibs[l, m, i] = out[(LINE + i) * SR : (LINE + i + 1) * SR]
+            sb_copy(l, m).start()
+
+    def add_cores(l, m):
+        sb_copy(l, m).wait_recv()
+        for i in (2, 1, 3, 0):
+            both = (own[l, m, i].astype(F32) + sibr[l, m, i].astype(F32)).astype(BF16)
             if i == 0:
-                gyr[l, 0] = both
+                gyr[l, m, 0] = both
             else:
-                gys[l, i] = both
-                gy_copy(l, i).start()
-
-    def place_columns(l):
-        for i in range(LINE):
+                gys[l, m, i] = both
+                gy_copy(l, m, i).start()
+
+    def place_columns(l, m):
+        for i in (0, 1, 3, 2):
             if i:
-                gy_copy(l, i).wait_recv()
+                gy_copy(l, m, i).wait_recv()
             k = (LINE - i) % LINE
             sel = one_hot((S, wide), shift_of[k], transposed=True)
-            out = dot(gyr[l, i].reshape(2 * SR, S), sel).astype(BF16)
+            out = dot(gyr[l, m, i], sel).astype(BF16)
             for q in range(wide // 128):
-                pad[l, i, q + 1] = out[:, q * 128 : (q + 1) * 128].reshape(2, SR, 128)
+                pad[l, m, i, q + 1] = out[:, q * 128 : (q + 1) * 128]
         per = CW // 128
         for q in range(C // 128):
             total = None
             for i in range(LINE):
                 k = (LINE - i) % LINE
                 at = jnp.clip(q - base_of[k], -1, wide // 128) + 1
-                term = pad[l, i, at].astype(F32)
+                term = pad[l, m, i, at].astype(F32)
                 total = term if total is None else total + term
-            canvas[l, q // per, :, :, (q % per) * 128 : (q % per + 1) * 128] = total.astype(BF16)
+            canvas[l, m, q // per, :, (q % per) * 128 : (q % per + 1) * 128] = total.astype(BF16)
         for d in range(1, n_pos):
-            ps_copy(l, d).start()
-
-    def finish(l):
-        total = canvas[l, p].astype(F32)
+            ps_copy(l, m, d).start()
+
+    def finish(l, m):
+        total = canvas[l, m, p].astype(F32)
         for d in range(1, n_pos):
-            ps_copy(l, d).wait_recv()
-            total = total + posr[l, d].astype(F32)
-        obj_out[l] = total
-
-    def gp_copy(i):
-        return copy(gps.at[i], gpr.at[i], gp_ss.at[i], gp_rs.at[i], ydev(i))
-
-    PR = S // n_pos
-
-    def gf_copy(d):
-        rows = pl.ds(pl.multiple_of(lax.rem(p + d, n_pos) * PR, PR), PR)
-        return copy(gsum.at[:, rows, :], gfr.at[d], gf_ss.at[d], gf_rs.at[d], pdev(d))
+            ps_copy(l, m, d).wait_recv()
+            total = total + posr[l, m, d].astype(F32)
+        obj_out[l, m] = total
+
+    def f1_copy(m, d, i):
+        src = gps.at[i, m, lax.rem(at_axis[m] + d, N)]
+        return copy(src, h1.at[m, d, i], f1_ss.at[m, d, i], f1_rs.at[m, d, i], axis_dev(m, d))
+
+    def f2_copy(m, d):
+        src = h.at[m, lax.rem(at_axis[1 - m] + d, N)]
+        return copy(src, h2.at[m, d], f2_ss.at[m, d], f2_rs.at[m, d], axis_dev(1 - m, d))
+
+    def f3_copy(i):
+        return copy(k2.at[i], k3.at[i], f3_ss.at[i], f3_rs.at[i], ydev(i))
+
+    def first_sum(m):
+        for i in range(LINE):
+            total = gps[i, m, at_axis[m]].astype(F32)
+            for d in range(1, N):
+                f1_copy(m, d, i).wait_recv()
+                total = total + h1[m, d, i].astype(F32)
+            for b in range(N):
+                h[m, b, i] = total[b].astype(BF16)
+        for d in range(1, N):
+            f2_copy(m, d).start()
+
+    def second_sum(m):
+        total = h[m, at_axis[1 - m]].astype(F32)
+        for d in range(1, N):
+            f2_copy(m, d).wait_recv()
+            total = total + h2[m, d].astype(F32)
+        for i in range(LINE):
+            k2[i, m] = total[i].astype(BF16)
 
     for n, i in enumerate((2, 1, 3, 0)):
         backward_a(i, n == 0)
     place_rows(1, g1)
+    for n, i in enumerate((2, 1, 3, 0)):
+        backward_b(i, n == 0)
+        for d in range(1, N):
+            for m in range(2):
+                f1_copy(m, d, i).start()
+        if n == 0:
+            add_cores(1, 0)
+            add_cores(1, 1)
+        if n == 2:
+            place_columns(1, 0)
+            place_columns(1, 1)
+    place_rows(0, g0)
+    add_cores(0, 0)
+    add_cores(0, 1)
+    first_sum(0)
+    first_sum(1)
+    place_columns(0, 0)
+    place_columns(0, 1)
+    second_sum(0)
+    second_sum(1)
+    for i in range(1, LINE):
+        f3_copy(i).start()
+    finish(1, 0)
+    finish(1, 1)
+    total = k2[0].astype(F32)
+    for i in range(1, LINE):
+        f3_copy(i).wait_recv()
+        total = total + k3[i].astype(F32)
+    prb_out[0] = total
+    finish(0, 0)
+    finish(0, 1)
+
+    for i in (1, 3):
+        p_copy(i).wait_send()
+    for i in range(1, LINE):
+        f3_copy(i).wait_send()
+        for l in range(layers):
+            w_copy(l, i).wait_send()
+            for m in range(2):
+                gy_copy(l, m, i).wait_send()
     for l in range(layers):
         for i in range(LINE):
-            pad[l, i, 0] = jnp.zeros((2, SR, 128), BF16)
-            pad[l, i, wide // 128 + 1] = jnp.zeros((2, SR, 128), BF16)
-    for n, i in enumerate((2, 1, 3, 0)):
-        backward_b(i, n == 0)
-        if i:
-            gp_copy(i).start()
-        if n == 0:
-            add_cores(1)
-        if n == 2:
-            place_columns(1)
-    place_rows(0, g0)
-    gp_copy(1).wait_recv()
-    gp_copy(3).wait_recv()
-    gp_copy(2).wait_recv()
-    for part in range(2):
-        total = gps[0, part].astype(F32)
-        for i in range(1, LINE):
-            total = total + gpr[i, part].astype(F32)
-        gsum[part] = total.astype(BF16)
-    for d in range(1, n_pos):
-        gf_copy(d).start()
-    add_cores(0)
-    place_columns(0)
-    finish(1)
-    my_rows = pl.ds(pl.multiple_of(p * PR, PR), PR)
-    total = gsum[:, my_rows, :].astype(F32)
-    for d in range(1, n_pos):
-        gf_copy(d).wait_recv()
-        total = total + gfr[d].astype(F32)
-    prb_out[0] = total
-    finish(0)
-
-    for i in range(1, LINE):
-        p_copy(i).wait_send()
-        gp_copy(i).wait_send()
-        for l in range(layers):
-            w_copy(l, i).wait_send()
-            gy_copy(l, i).wait_send()
-    for l in range(layers):
-        sb_copy(l).wait_send()
-        for i in range(LINE):
             relay(l, i).wait_send()
-        for d in range(1, n_pos):
-            ps_copy(l, d).wait_send()
+        for m in range(2):
+            sb_copy(l, m).wait_send()
+            for d in range(1, n_pos):
+                ps_copy(l, m, d).wait_send()
     for d in range(1, n_pos):
         a_copy(d).wait_send()
-        gf_copy(d).wait_send()
+    for m in range(2):
+        p_pass(m).wait_send()
+        for d in range(1, N):
+            f2_copy(m, d).wait_send()
+            for i in range(LINE):
+                f1_copy(m, d, i).wait_send()
     pw_c.wait_send()
     ah_c.wait_send()
 
@@ -393,7 +462,15 @@
     wide = S + 128
     vm = pltpu.VMEM
     dma = pltpu.SemaphoreType.DMA
+    PR = S // n_pos
+    N = math.isqrt(n_pos)
     scratch = [
+        vm(probe_modes.shape, F32),
+        vm(object_slices.shape, BF16),
+        vm(amplitudes.shape, BF16),
+        vm((2 * S, 2 * S), BF16),
+        vm((2 * S, 2 * S), BF16),
+        vm((2, S, S), F32),
         vm((layers, C // 128, 2 * SR, 128), BF16),
         vm((layers, LINE, 2, SR, S), BF16),
         vm((layers, 2, RW, S), BF16),
@@ -410,22 +487,25 @@
         vm((LINE, 2 * S, S), BF16),
         vm((2, S, S), F32),
         vm((2, S, S), F32),
-        vm((layers, LINE, 2, SR, S), BF16),
-        vm((layers, LINE, 2, SR, S), BF16),
-        vm((layers, LINE, 2, SR, S), BF16),
-        vm((layers, LINE, 2, SR, S), BF16),
-        vm((layers, LINE, 2, SR, S), BF16),
-        vm((layers, LINE, wide // 128 + 2, 2, SR, 128), BF16),
-        vm((layers, n_pos, 2, SR, CW), BF16),
-        vm((layers, n_pos, 2, SR, CW), BF16),
-        vm((LINE, 2, S, S), BF16),
-        vm((LINE, 2, S, S), BF16),
-        vm((2, S, S), BF16),
-        vm((n_pos, 2, S // n_pos, S), BF16),
+        vm((layers, 2, LINE, SR, S), BF16),
+        vm((layers, 2, LINE, SR, S), BF16),
+        vm((layers, 2, LINE, SR, S), BF16),
+        vm((layers, 2, LINE, SR, S), BF16),
+        vm((layers, 2, LINE, SR, S), BF16),
+        vm((layers, 2, LINE, wide // 128 + 2, SR, 128), BF16),
+        vm((layers, 2, n_pos, SR, CW), BF16),
+        vm((layers, 2, n_pos, SR, CW), BF16),
+        vm((LINE, 2, N, N, PR, S), BF16),
+        vm((2, N, LINE, N, PR, S), BF16),
+        vm((2, N, LINE, PR, S), BF16),
+        vm((2, N, LINE, PR, S), BF16),
+        vm((LINE, 2, PR, S), BF16),
+        vm((LINE, 2, PR, S), BF16),
+        dma((6,)),
     ]
     for shape in (
         (layers, LINE), (layers, LINE), (LINE,), (n_pos,), (1,), (1,),
-        (layers,), (layers, LINE), (layers, n_pos), (LINE,), (n_pos,),
+        (layers, 2), (layers, 2, LINE), (layers, 2, n_pos), (2, N, LINE), (2, N), (LINE,),
     ):
         scratch += [dma(shape), dma(shape)]
     smem = pl.BlockSpec(memory_space=pltpu.SMEM)
@@ -436,14 +516,14 @@
             jax.ShapeDtypeStruct((layers, 2, SR, CW), F32),
             jax.ShapeDtypeStruct((1, 2, S // n_pos, S), F32),
         ),
-        in_specs=[smem, smem] + [vmem] * 6,
+        in_specs=[smem, smem] + [pl.BlockSpec(memory_space=pltpu.HBM)] * 6,
         out_specs=(vmem, vmem),
         scratch_shapes=scratch,
         compiler_params=pltpu.CompilerParams(
             collective_id=0, has_side_effects=True, vmem_limit_bytes=60 * 1024 * 1024
         ),
         name="ptycho",
-    )(slot_counts, scan_offsets, probe_modes, object_slices, amplitudes, *consts)
+    )(slot_counts, scan_offsets.T, probe_modes, object_slices, amplitudes, *consts)
 
 
 def solution(mesh):

time: 78.9 us -> 64.3 us (0.81)
  Pallas kernels: 74.5 us -> 61.4 us
  local copies, waits for them, and re-layouts: 3.61 us -> 2.19 us
    pallas_call x1, Pallas kernels: 74.5 us -> 61.4 us  [on_device(): pl.pallas_call(functools.partial(body, n_pos=n_pos), out_shape=(jax.Shape...]
    unnamed x5 -> x4, local copies, waits for them, and re-layouts: 3.61 us -> 2.19 us
where the time goes in v2:
time: 64.3 us; the launch traced here: 64.2 us
  Pallas kernels  61.4 us (95%)
  local copies, waits for them, and re-layouts  2.19 us (3%)
  between operations  0.65 us (1%)
    pallas_call x1, Pallas kernels, on_device(): pl.pallas_call(functools.partial(body, n_pos=n_pos), out_shape=(jax.Shape...  61.4 us
    unnamed x4, local copies, waits for them, and re-layouts  2.19 us

profile of v2, /device:TPU:0, one launch (start us, length us, event | category | flops | bytes accessed | tf_op | source)
XLA Modules:
  0.0 64.2 jit_solution(8869912292871431853)
XLA Ops:
  0.6 61.4 %ptycho.1 = (f32[2,2,64,128]{3,2,1,0:T(8,128)}, f32[1,2,16,256]{3,2,1,0:T(8,128)}) custom-call(s32[16]{0:T(128)} %counts.1, s32[2,128]{1,0:T(2,128)} %bitcast.1, f32[1,2,256,256]{3,2,1,0:T(8,128)} %probe_in.1, bf16[2,2,64,2048]{3,2,1,0:T(8,128)(2,1)} %strip_in.1, bf16[8,256,256]{2,1,0:T(8,128)(2,1)} %amp_in.1, bf16[512,512]{1,0:T(8,128)(2,1)} %constant.6.clone.amat_in, ...), custom_call_target="tpu_custom_call" | custom-call | tf_op jit(solution)/shard_map/ptycho/pallas_call | solution.py:513
  62.0 0.0 copy-start
  62.0 1.6 %copy.12 = f32[2,2,64,128]{3,2,1,0:T(8,128)} copy(f32[2,2,64,128]{3,2,1,0:T(8,128)} %get-tuple-element.4) | data formatting | bytes 262144
  63.6 0.0 copy-done
  63.6 0.6 copy.13
Async XLA Ops:
  62.0 1.6 %copy-start = (f32[1,2,16,256]{3,2,1,0:T(8,128)S(1)}, f32[1,2,16,256]{3,2,1,0:T(8,128)}, u32[]{:S(2)}) copy-start(f32[1,2,16,256]{3,2,1,0:T(8,128)} %get-tuple-element.5) | copy-start | bytes 98308
